TPU v7x, 32 devices: a whole 2x2x4 slice. The times are simulated.
32 devices in a mesh: depth: 2 (over core), rows: 2 (over x), shots: 8 (over z, y).
Axes of the slice: x: 2, y: 2, z: 4, core: 2. Of those that a mesh axis runs over, the one named last changes fastest.
Arguments:
- sources: float32 [2, 2, 1024, 1024], P('depth', None, 'rows', 'shots'), may hold values from -6 to 6
- factor: float32 [2, 2, 1024, 1024], P('depth', None, ('rows', 'shots')), may hold values from -0.09375 to 0.09375
- block_mask: int32 [2, 2, 8, 8], P('depth'), may hold values 0 or 1
- inverse_diagonal: float32 [2, 2, 1024, 1024], P('depth', None, None, 'rows'), may hold values from -1.2 to 1.2, as said below
Outputs:
- solution: float32 [2, 2, 1024, 1024], P('depth', None, 'rows', 'shots')
Inputs may be any that keep to these rules, and one draw needn't show every extreme that they name: Each block inverse_diagonal[d, m] is lower triangular with diagonal entries between 0.8 and 1.2.
All inputs are finite; a program needn't handle non-finite values. No bound on the sum of `block_mask` on one device may be relied on, other than what follows from the above.
Results may differ from a plain program's by a relative error of at most 0.0001.
Values sent between devices are 32-bit elements; how exact they have to be, the bound alone decides.
No kernel may reach another device: no remote copies, remote signals or barrier semaphores. Data moves between devices by JAX's collectives and lax.ppermute only.
A program may use at most 64 MiB of HBM per device.

v0:
```python
import jax
import jax.numpy as jnp
from jax import lax
from jax.sharding import PartitionSpec as P


def mask_rows(factor_rows, block_mask, row_start, block_size):
    row_total = factor_rows.shape[1]
    block_count = block_mask.shape[3]
    row_blocks = (row_start + jnp.arange(row_total, dtype=jnp.int32)) // block_size
    row_select = (row_blocks[:, None] == jnp.arange(block_count, dtype=jnp.int32)[None, :]).astype(
        jnp.float32
    )
    row_masks = jnp.einsum("rk,pkc->prc", row_select, block_mask[0].astype(jnp.float32))
    return factor_rows * jnp.repeat(row_masks, block_size, axis=2)


def group_reduce(partial_value):
    summed = lax.psum_scatter(partial_value, "depth", scatter_dimension=0, tiled=True)
    return summed[0]


def group_collect(spread):
    every_rows = lax.all_gather(spread[None], "depth", axis=0, tiled=True)
    return every_rows


def invert_level(inverse_block, own_rows):
    inverse_term = jnp.dot(
        inverse_block, own_rows, precision=lax.Precision.HIGHEST, preferred_element_type=jnp.float32
    )
    return lax.psum(inverse_term, "rows")


def per_device(sources, factor, block_mask, inverse_diagonal):
    depth_count = lax.axis_size("depth")
    tree_height = depth_count.bit_length() - 1
    level_count = tree_height + 1
    rows_index = lax.axis_index("rows")
    full_width = factor.shape[3]
    block_count = block_mask.shape[3]
    block_size = full_width // block_count
    highest = lax.Precision.HIGHEST
    front_factor = lax.all_gather(factor[0], "shots", axis=1, tiled=True)
    front_count = front_factor.shape[1]
    masked = mask_rows(front_factor, block_mask, rows_index * front_count, block_size)
    solved = []
    for tier_index in range(level_count):
        own_rows = sources[0, tier_index]
        if tier_index > 0:
            group_size = 2**tier_index
            factor_tiles = masked.reshape(tier_index, group_size, front_count, full_width)
            lower_solved = jnp.stack(solved[:tier_index])
            partial_value = jnp.einsum(
                "lgrs,lsn->grn",
                factor_tiles,
                lower_solved,
                precision=highest,
                preferred_element_type=jnp.float32,
            )
            reduced = group_reduce(partial_value)
            own_rows = own_rows - reduced
        full_rows = invert_level(inverse_diagonal[0, tier_index], own_rows)
        solved.append(full_rows)
    answers = [None] * level_count
    collected = {}
    for tier_index in reversed(range(level_count)):
        target = solved[tier_index]
        if tier_index < tree_height:
            factor_tiles = masked
            transposed = jnp.einsum(
                "grs,grn->sn",
                factor_tiles,
                collected[1],
                precision=highest,
                preferred_element_type=jnp.float32,
            )
            own_columns = lax.psum(transposed, "rows")
            target = target - own_columns
        answer = lax.dot_general(
            inverse_diagonal[0, tier_index],
            target,
            (((0,), (0,)), ((), ())),
            precision=highest,
            preferred_element_type=jnp.float32,
        )
        answers[tier_index] = answer
        if tier_index > 0:
            collected[tier_index] = group_collect(answer)
    return jnp.stack(answers)[None]


def solution(mesh):
    placed = (
        P("depth", None, "rows", "shots"),
        P("depth", None, ("rows", "shots"), None),
        P("depth", None, None, None),
        P("depth", None, None, "rows"),
    )
    return jax.shard_map(
        per_device,
        mesh=mesh,
        in_specs=placed,
        out_specs=P("depth", None, "rows", "shots"),
        check_vma=False,
    )
```

profile of v0, /device:TPU:0, one launch (start us, length us, event | category | flops | bytes accessed | tf_op | source)
XLA Modules:
  0.0 194.4 jit_solution(14296305653696996673)
XLA Ops:
  7.4 0.0 all-reduce.4.cloned.1.call-start
  7.4 4.2 %fusion.6 = f32[1024,128]{1,0:T(8,128)} fusion(f32[1,2,1024,512]{3,2,1,0:T(8,128)} %param.7, f32[1,2,512,128]{3,2,1,0:T(8,128)} %param.4), kind=kOutput, calls=%fused_computation.7 | convolution fusion | flops 805306368 | bytes 2883584 | tf_op jit(solution)/shard_map/dot_general | solution.py:29
  11.5 0.0 all-reduce.4.cloned.1.call-update
  11.6 0.0 all-gather.4.cloned.1.call-start
  11.6 0.5 all-gather.4.cloned.1.call-update
  12.2 0.0 reduce-scatter.2.cloned.1.call-start
  12.2 0.7 convert_bitcast_fusion
  12.9 0.1 copy.5
  13.0 0.1 convolution_bitcast_fusion
  13.1 0.2 copy.6
  13.3 2.6 %broadcast_in_dim.11 = f32[2,512,8,128]{3,2,1,0:T(8,128)} broadcast(f32[2,512,8]{2,1,0:T(8,128)S(1)} %copy.6), dimensions={0,1,2} | broadcast | bytes 4227072 | tf_op jit(solution)/shard_map/broadcast_in_dim | solution.py:15
  15.9 4.9 %reshape.30 = f32[2,512,1024]{2,1,0:T(8,128)} reshape(f32[2,512,8,128]{3,2,1,0:T(8,128)} %broadcast_in_dim.11) | data formatting | bytes 8388608 | tf_op jit(solution)/shard_map/reshape | solution.py:15
  20.8 0.0 copy-start.1
  20.8 22.3 %all-reduce.4.cloned.1.call-done = f32[1024,128]{1,0:T(8,128)} async-done(((f32[1024,128]{1,0:T(8,128)}), f32[1024,128]{1,0:T(8,128)}) %all-reduce.4.cloned.1.call-update) | async-done | bytes 524304 | tf_op jit(solution)/shard_map/psum | solution.py:32
  43.1 46.4 %all-gather.4.cloned.1.call-done = f32[1,2,512,1024]{3,2,1,0:T(8,128)} async-done(((f32[1,2,64,1024]{3,2,1,0:T(8,128)}), f32[1,2,512,1024]{3,2,1,0:T(8,128)}) %all-gather.4.cloned.1.call-update) | async-done | bytes 4194320 | tf_op jit(solution)/shard_map/all_gather | solution.py:44
  89.5 7.7 %fusion.13 = f32[2,512,128]{2,1,0:T(8,128)} fusion(f32[2,512,1024]{2,1,0:T(8,128)} %reshape.30, f32[1,2,512,1024]{3,2,1,0:T(8,128)} %all-gather.4.cloned.1.call-done, f32[1024,128]{1,0:T(8,128)} %all-reduce.4.cloned.1.call-done), kind=kOutput, calls=%fused_computation.14 | convolution fusion | flops 1611661312 | bytes 9437184 | tf_op jit(solution)/shard_map/lgrs,lsn->grn/dot_general | solution.py:54
  97.2 0.0 reduce-scatter.2.cloned.1.call-update
  97.3 0.0 all-reduce.6.cloned.1.call-start
  97.3 6.6 %reduce-scatter.2.cloned.1.call-done = f32[1,512,128]{2,1,0:T(8,128)} async-done(((f32[2,512,128]{2,1,0:T(8,128)}), f32[1,512,128]{2,1,0:T(8,128)}) %reduce-scatter.2.cloned.1.call-update) | async-done | bytes 262160 | tf_op jit(solution)/shard_map/reduce_scatter | solution.py:19
  103.9 0.0 copy-done.1
  103.9 4.8 %fusion.15 = f32[1024,128]{0,1:T(8,128)} fusion(f32[1,2,1024,512]{3,2,1,0:T(8,128)} %param.7, f32[1,512,128]{2,1,0:T(8,128)} %reduce-scatter.2.cloned.1.call-done, f32[1,2,512,128]{3,2,1,0:T(8,128)S(1)} %copy-done.1), kind=kOutput, calls=%fused_computation.16 | convolution fusion | flops 805371904 | bytes 3145728 | tf_op jit(solution)/shard_map/dot_general | solution.py:29
  108.7 0.0 all-reduce.6.cloned.1.call-update
  108.7 0.0 all-reduce.8.cloned.1.call-start
  108.8 29.9 %all-reduce.6.cloned.1.call-done = f32[1024,128]{0,1:T(8,128)} async-done(((f32[1024,128]{0,1:T(8,128)}), f32[1024,128]{0,1:T(8,128)}) %all-reduce.6.cloned.1.call-update) | async-done | bytes 524304 | tf_op jit(solution)/shard_map/psum | solution.py:32
  138.7 3.1 %fusion = f32[128,512]{1,0:T(8,128)S(1)} fusion(f32[1024,128]{0,1:T(8,128)} %all-reduce.6.cloned.1.call-done, f32[1,2,1024,512]{3,2,1,0:T(8,128)} %param.7), kind=kOutput, calls=%fused_computation.1 | convolution fusion | flops 805306368 | bytes 2883584 | tf_op jit(solution)/shard_map/dot_general | solution.py:80
  141.7 2.4 %all-gather.1 = f32[1024,128]{0,1:T(8,128)S(1)} all-gather(f32[512,128]{0,1:T(8,128)S(1)} %bitcast.63), channel_id=3, replica_groups=mesh['depth'=2,'rows'=2,'shots'=8] {'depth'}, dimensions={0}, use_global_device_ids=true | all-gather | bytes 786432 | tf_op jit(solution)/shard_map/all_gather | solution.py:24
  144.1 0.2 copy.9
  144.3 0.0 copy-start
  144.3 10.0 %fusion.14 = f32[1024,128]{1,0:T(8,128)} fusion(f32[2,512,128]{2,1,0:T(8,128)S(1)} %bitcast.65, f32[2,512,1024]{2,1,0:T(8,128)} %reshape.30, f32[1,2,512,1024]{3,2,1,0:T(8,128)} %all-gather.4.cloned.1.call-done), kind=kOutput, calls=%fused_computation.15 | convolution fusion | flops 1611661312 | bytes 9437184 | tf_op jit(solution)/shard_map/grs,grn->sn/dot_general | solution.py:71
  154.3 0.0 all-reduce.8.cloned.1.call-update
  154.3 28.8 %all-reduce.8.cloned.1.call-done = f32[1024,128]{1,0:T(8,128)} async-done(((f32[1024,128]{1,0:T(8,128)}), f32[1024,128]{1,0:T(8,128)}) %all-reduce.8.cloned.1.call-update) | async-done | bytes 524304 | tf_op jit(solution)/shard_map/psum | solution.py:78
  183.1 0.0 copy-done
  183.1 3.2 %fusion.18 = f32[1,512,128]{1,2,0:T(8,128)S(1)} fusion(f32[1,2,1024,512]{3,2,1,0:T(8,128)} %param.7, f32[1024,128]{1,0:T(8,128)S(1)} %copy-done, f32[1024,128]{1,0:T(8,128)} %all-reduce.8.cloned.1.call-done), kind=kOutput, calls=%fused_computation.17 | convolution fusion | flops 805437440 | bytes 3407872 | tf_op jit(solution)/shard_map/dot_general | solution.py:80
  186.3 1.0 copy.7
  (2 shorter events, 0.0 us)
Async XLA Ops:
  7.4 35.7 %all-reduce.4.cloned.1.call-start = ((), (), s32[]{:S(2)}) async-start(), calls=%async_computation.1 | async-start | bytes 1048576 | tf_op jit(solution)/shard_map/psum | solution.py:32
  11.6 78.0 %all-gather.4.cloned.1.call-start = ((), (), s32[]{:S(2)}) async-start(), calls=%async_computation.5 | async-start | bytes 4718592 | tf_op jit(solution)/shard_map/all_gather | solution.py:44
  12.2 91.8 %reduce-scatter.2.cloned.1.call-start = ((), (), s32[]{:S(2)}) async-start(), calls=%async_computation.2 | async-start | bytes 786432 | tf_op jit(solution)/shard_map/reduce_scatter | solution.py:19
  20.8 83.1 %copy-start.1 = (f32[1,2,512,128]{3,2,1,0:T(8,128)S(1)}, f32[1,2,512,128]{3,2,1,0:T(8,128)}, u32[]{:S(2)}) copy-start(f32[1,2,512,128]{3,2,1,0:T(8,128)} %param.4) | copy-start | bytes 1572868
  97.3 41.4 %all-reduce.6.cloned.1.call-start = ((), (), s32[]{:S(2)}) async-start(), calls=%async_computation.3 | async-start | bytes 1048576 | tf_op jit(solution)/shard_map/psum | solution.py:32
  108.7 74.3 %all-reduce.8.cloned.1.call-start = ((), (), s32[]{:S(2)}) async-start(), calls=%async_computation.4 | async-start | bytes 1048576 | tf_op jit(solution)/shard_map/psum | solution.py:78
  144.3 38.8 %copy-start = (f32[1024,128]{1,0:T(8,128)S(1)}, f32[1024,128]{1,0:T(8,128)}, u32[]{:S(2)}) copy-start(f32[1024,128]{1,0:T(8,128)} %all-reduce.4.cloned.1.call-done) | copy-start | bytes 1572868
Sparse Core Ops, SparseCore 0:
  11.7 31.3 all-reduce.3
  97.4 6.5 reduce-scatter.1
  108.9 29.7 all-reduce.5
  154.4 28.6 all-reduce.7
Sparse Core Ops, SparseCore 1:
  14.2 75.2 all-gather.3
where the time goes:
time: 195 us; the launch traced here: 194 us
  waiting for transfers between devices  135 us (69%)
  matrix products  33 us (17%)
  between operations  14.6 us (7%)
  local copies, waits for them, and re-layouts  8.97 us (5%)
  blocking collectives  2.36 us (1%)
    psum x2, waiting for transfers between devices, invert_level(): return lax.psum(inverse_term, 'rows')  52.1 us
    all_gather x1, waiting for transfers between devices, per_device(): front_factor = lax.all_gather(factor[0], 'shots', axis=1, tiled=True)  46.4 us
    psum x1, waiting for transfers between devices, per_device(): own_columns = lax.psum(transposed, 'rows')  28.8 us
    dot_general x1, matrix products, per_device(): jnp.einsum('grs,grn->sn', factor_tiles, collected[1], precision=highest,...  9.96 us
    dot_general x2, matrix products, invert_level(): jnp.dot(inverse_block, own_rows, precision=lax.Precision.HIGHEST, preferr...  8.97 us
    dot_general x1, matrix products, per_device(): jnp.einsum('lgrs,lsn->grn', factor_tiles, lower_solved, precision=highest...  7.7 us
    reduce_scatter x1, waiting for transfers between devices, group_reduce(): lax.psum_scatter(partial_value, 'depth', scatter_dimension=0, tiled=True)  6.63 us
    dot_general x2, matrix products, per_device(): lax.dot_general(inverse_diagonal[0, tier_index], target, (((0,), (0,)), (...  6.22 us
  transfers between devices with their start and end apart: 5, of which 5 were waited for; matrix products, arithmetic and copies ran while one was open for 4% of the time, Pallas kernels for 0%

commit v1 on v0

--- a/solution.py
+++ b/solution.py
@@ -2,6 +2,11 @@
 import jax.numpy as jnp
 from jax import lax
 from jax.sharding import PartitionSpec as P
+
+
+def summed_here(x, name):
+    shards = lax.all_gather(x, name)
+    return jnp.sum(shards, axis=0)
 
 
 def mask_rows(factor_rows, block_mask, row_start, block_size):
@@ -75,7 +80,7 @@
                 precision=highest,
                 preferred_element_type=jnp.float32,
             )
-            own_columns = lax.psum(transposed, "rows")
+            own_columns = summed_here(transposed, "rows")
             target = target - own_columns
         answer = lax.dot_general(
             inverse_diagonal[0, tier_index],

time: 195 us -> 189 us (0.969)
  waiting for transfers between devices: 135 us -> 127 us
    psum x1 -> x0, waiting for transfers between devices: 28.8 us -> none  [per_device(): own_columns = lax.psum(transposed, 'rows')]
    all_gather x0 -> x1, waiting for transfers between devices: none -> 21.4 us  [summed_here(): shards = lax.all_gather(x, name)]
  transfers between devices with their start and end apart: 5 -> 5, of which waited for: 5 -> 5; matrix products, arithmetic and copies ran while one was open for 4% -> 5% of each run, Pallas kernels for 0% -> 0%
where the time goes in v1:
time: 189 us; the launch traced here: 188 us
  waiting for transfers between devices  127 us (67%)
  matrix products  32.8 us (17%)
  between operations  14.6 us (8%)
  local copies, waits for them, and re-layouts  8.97 us (5%)
  blocking collectives  2.36 us (1%)
  other arithmetic  2.09 us (1%)
    psum x2, waiting for transfers between devices, invert_level(): return lax.psum(inverse_term, 'rows')  52.1 us
    all_gather x1, waiting for transfers between devices, per_device(): front_factor = lax.all_gather(factor[0], 'shots', axis=1, tiled=True)  46.4 us
    all_gather x1, waiting for transfers between devices, summed_here(): shards = lax.all_gather(x, name)  21.4 us
    dot_general x1, matrix products, per_device(): jnp.einsum('grs,grn->sn', factor_tiles, collected[1], precision=highest,...  9.96 us
    dot_general x2, matrix products, invert_level(): jnp.dot(inverse_block, own_rows, precision=lax.Precision.HIGHEST, preferr...  8.97 us
    dot_general x1, matrix products, per_device(): jnp.einsum('lgrs,lsn->grn', factor_tiles, lower_solved, precision=highest...  7.7 us
    reduce_scatter x1, waiting for transfers between devices, group_reduce(): lax.psum_scatter(partial_value, 'depth', scatter_dimension=0, tiled=True)  6.63 us
    dot_general x2, matrix products, per_device(): lax.dot_general(inverse_diagonal[0, tier_index], target, (((0,), (0,)), (...  6.04 us
  transfers between devices with their start and end apart: 5, of which 5 were waited for; matrix products, arithmetic and copies ran while one was open for 5% of the time, Pallas kernels for 0%

profile of v1, /device:TPU:0, one launch (start us, length us, event | category | flops | bytes accessed | tf_op | source)
XLA Modules:
  0.0 188.2 jit_solution(5667522238775290834)
XLA Ops:
  7.4 0.0 all-reduce.3.cloned.1.call-start
  7.4 4.2 %fusion.6 = f32[1024,128]{1,0:T(8,128)} fusion(f32[1,2,1024,512]{3,2,1,0:T(8,128)} %param.7, f32[1,2,512,128]{3,2,1,0:T(8,128)} %param.4), kind=kOutput, calls=%fused_computation.7 | convolution fusion | flops 805306368 | bytes 2883584 | tf_op jit(solution)/shard_map/dot_general | solution.py:34
  11.5 0.0 all-reduce.3.cloned.1.call-update
  11.6 0.0 all-gather.6.cloned.1.call-start
  11.6 0.5 all-gather.6.cloned.1.call-update
  12.2 0.0 reduce-scatter.2.cloned.1.call-start
  12.2 0.7 convert_bitcast_fusion
  12.9 0.1 copy.5
  13.0 0.1 convolution_bitcast_fusion
  13.1 0.2 copy.6
  13.3 2.6 %broadcast_in_dim.11 = f32[2,512,8,128]{3,2,1,0:T(8,128)} broadcast(f32[2,512,8]{2,1,0:T(8,128)S(1)} %copy.6), dimensions={0,1,2} | broadcast | bytes 4227072 | tf_op jit(solution)/shard_map/broadcast_in_dim | solution.py:20
  15.9 4.9 %reshape.30 = f32[2,512,1024]{2,1,0:T(8,128)} reshape(f32[2,512,8,128]{3,2,1,0:T(8,128)} %broadcast_in_dim.11) | data formatting | bytes 8388608 | tf_op jit(solution)/shard_map/reshape | solution.py:20
  20.8 0.0 copy-start.1
  20.8 22.3 %all-reduce.3.cloned.1.call-done = f32[1024,128]{1,0:T(8,128)} async-done(((f32[1024,128]{1,0:T(8,128)}), f32[1024,128]{1,0:T(8,128)}) %all-reduce.3.cloned.1.call-update) | async-done | bytes 524304 | tf_op jit(solution)/shard_map/psum | solution.py:37
  43.1 46.4 %all-gather.6.cloned.1.call-done = f32[1,2,512,1024]{3,2,1,0:T(8,128)} async-done(((f32[1,2,64,1024]{3,2,1,0:T(8,128)}), f32[1,2,512,1024]{3,2,1,0:T(8,128)}) %all-gather.6.cloned.1.call-update) | async-done | bytes 4194320 | tf_op jit(solution)/shard_map/all_gather | solution.py:49
  89.5 7.7 %fusion.13 = f32[2,512,128]{2,1,0:T(8,128)} fusion(f32[2,512,1024]{2,1,0:T(8,128)} %reshape.30, f32[1,2,512,1024]{3,2,1,0:T(8,128)} %all-gather.6.cloned.1.call-done, f32[1024,128]{1,0:T(8,128)} %all-reduce.3.cloned.1.call-done), kind=kOutput, calls=%fused_computation.14 | convolution fusion | flops 1611661312 | bytes 9437184 | tf_op jit(solution)/shard_map/lgrs,lsn->grn/dot_general | solution.py:59
  97.2 0.0 reduce-scatter.2.cloned.1.call-update
  97.3 0.0 all-reduce.5.cloned.1.call-start
  97.3 6.6 %reduce-scatter.2.cloned.1.call-done = f32[1,512,128]{2,1,0:T(8,128)} async-done(((f32[2,512,128]{2,1,0:T(8,128)}), f32[1,512,128]{2,1,0:T(8,128)}) %reduce-scatter.2.cloned.1.call-update) | async-done | bytes 262160 | tf_op jit(solution)/shard_map/reduce_scatter | solution.py:24
  103.9 0.0 copy-done.1
  103.9 4.8 %fusion.15 = f32[1024,128]{0,1:T(8,128)} fusion(f32[1,2,1024,512]{3,2,1,0:T(8,128)} %param.7, f32[1,512,128]{2,1,0:T(8,128)} %reduce-scatter.2.cloned.1.call-done, f32[1,2,512,128]{3,2,1,0:T(8,128)S(1)} %copy-done.1), kind=kOutput, calls=%fused_computation.16 | convolution fusion | flops 805371904 | bytes 3145728 | tf_op jit(solution)/shard_map/dot_general | solution.py:34
  108.7 0.0 all-reduce.5.cloned.1.call-update
  108.7 0.0 all-gather.8.cloned.1.call-start
  108.8 29.9 %all-reduce.5.cloned.1.call-done = f32[1024,128]{0,1:T(8,128)} async-done(((f32[1024,128]{0,1:T(8,128)}), f32[1024,128]{0,1:T(8,128)}) %all-reduce.5.cloned.1.call-update) | async-done | bytes 524304 | tf_op jit(solution)/shard_map/psum | solution.py:37
  138.7 3.1 %fusion = f32[128,512]{1,0:T(8,128)S(1)} fusion(f32[1024,128]{0,1:T(8,128)} %all-reduce.5.cloned.1.call-done, f32[1,2,1024,512]{3,2,1,0:T(8,128)} %param.7), kind=kOutput, calls=%fused_computation.1 | convolution fusion | flops 805306368 | bytes 2883584 | tf_op jit(solution)/shard_map/dot_general | solution.py:85
  141.7 2.4 %all-gather.1 = f32[1024,128]{0,1:T(8,128)S(1)} all-gather(f32[512,128]{0,1:T(8,128)S(1)} %bitcast.64), channel_id=3, replica_groups=mesh['depth'=2,'rows'=2,'shots'=8] {'depth'}, dimensions={0}, use_global_device_ids=true | all-gather | bytes 786432 | tf_op jit(solution)/shard_map/all_gather | solution.py:29
  144.1 0.2 copy.11
  144.3 0.0 copy-start
  144.3 10.0 %fusion.14 = f32[1024,128]{1,0:T(8,128)} fusion(f32[2,512,128]{2,1,0:T(8,128)S(1)} %bitcast.66, f32[2,512,1024]{2,1,0:T(8,128)} %reshape.30, f32[1,2,512,1024]{3,2,1,0:T(8,128)} %all-gather.6.cloned.1.call-done), kind=kOutput, calls=%fused_computation.15 | convolution fusion | flops 1611661312 | bytes 9437184 | tf_op jit(solution)/shard_map/grs,grn->sn/dot_general | solution.py:76
  154.3 0.0 all-gather.8.cloned.1.call-update
  154.3 21.4 %all-gather.8.cloned.1.call-done = f32[2048,128]{1,0:T(8,128)} async-done(((f32[1024,128]{1,0:T(8,128)}), f32[2048,128]{1,0:T(8,128)}) %all-gather.8.cloned.1.call-update) | async-done | bytes 1048592 | tf_op jit(solution)/shard_map/all_gather | solution.py:8
  175.7 1.3 reduce_sum.9
  177.1 0.0 copy-done
  177.1 3.0 %fusion.18 = f32[1,512,128]{1,2,0:T(8,128)S(1)} fusion(f32[1,2,1024,512]{3,2,1,0:T(8,128)} %param.7, f32[1024,128]{1,0:T(8,128)S(1)} %copy-done, f32[1024,128]{1,0:T(8,128)S(1)} %reduce_sum.9), kind=kOutput, calls=%fused_computation.17 | convolution fusion | flops 805437440 | bytes 3407872 | tf_op jit(solution)/shard_map/dot_general | solution.py:85
  180.1 1.0 copy.9
  (2 shorter events, 0.0 us)
Async XLA Ops:
  7.4 35.7 %all-reduce.3.cloned.1.call-start = ((), (), s32[]{:S(2)}) async-start(), calls=%async_computation.1 | async-start | bytes 1048576 | tf_op jit(solution)/shard_map/psum | solution.py:37
  11.6 78.0 %all-gather.6.cloned.1.call-start = ((), (), s32[]{:S(2)}) async-start(), calls=%async_computation.4 | async-start | bytes 4718592 | tf_op jit(solution)/shard_map/all_gather | solution.py:49
  12.2 91.8 %reduce-scatter.2.cloned.1.call-start = ((), (), s32[]{:S(2)}) async-start(), calls=%async_computation.2 | async-start | bytes 786432 | tf_op jit(solution)/shard_map/reduce_scatter | solution.py:24
  20.8 83.1 %copy-start.1 = (f32[1,2,512,128]{3,2,1,0:T(8,128)S(1)}, f32[1,2,512,128]{3,2,1,0:T(8,128)}, u32[]{:S(2)}) copy-start(f32[1,2,512,128]{3,2,1,0:T(8,128)} %param.4) | copy-start | bytes 1572868
  97.3 41.4 %all-reduce.5.cloned.1.call-start = ((), (), s32[]{:S(2)}) async-start(), calls=%async_computation.3 | async-start | bytes 1048576 | tf_op jit(solution)/shard_map/psum | solution.py:37
  108.7 67.0 %all-gather.8.cloned.1.call-start = ((), (), s32[]{:S(2)}) async-start(), calls=%async_computation.5 | async-start | bytes 1572864 | tf_op jit(solution)/shard_map/all_gather | solution.py:8
  144.3 32.8 %copy-start = (f32[1024,128]{1,0:T(8,128)S(1)}, f32[1024,128]{1,0:T(8,128)}, u32[]{:S(2)}) copy-start(f32[1024,128]{1,0:T(8,128)} %all-reduce.3.cloned.1.call-done) | copy-start | bytes 1572868
Sparse Core Ops, SparseCore 0:
  11.7 31.3 all-reduce.2
  97.4 6.5 reduce-scatter.1
  108.9 29.7 all-reduce.4
  154.4 21.2 all-gather.7
Sparse Core Ops, SparseCore 1:
  14.2 75.2 all-gather.5
